TPU v7x, 32 devices: a whole 2x2x4 slice. The times are simulated.
32 devices in a mesh: batch: 8 (over z, core), vocab: 4 (over y, x).
Axes of the slice: x: 2, y: 2, z: 4, core: 2. Of those that a mesh axis runs over, the one named last changes fastest.
Arguments:
- hidden: bfloat16 [1024, 4096], P('batch'), may hold values from -40 to 40
- exit_layer: int32 [1024], P('batch'), may hold values from 0 to 7
- exit_gains: float32 [8, 4096], replicated, may hold values from 0.1 to 1.9
- unembed: bfloat16 [4096, 128256], P(None, ('batch', 'vocab')), may hold values from -10 to 10
- targets: int32 [1024], replicated, may hold values from 0 to 128255
- values: float32 [1024], P('batch'), may hold values from -6 to 6
- rewards: float32 [1024], P('batch'), may hold values from -2 to 2
- ref_logprob: float32 [1024], P('batch'), may hold values from -16 to -6
- segment_end: int32 [1024], P('batch'), may hold values 0 or 1
Outputs:
- logprob: float32 [1024], P('batch')
- advantages: float32 [1024], P('batch')
All inputs are finite; a program needn't handle non-finite values. No bound on the sum of `segment_end` on one device may be relied on, other than what follows from the above.
Results may differ from a plain program's by a relative error of at most 0.00054.
Values may be sent and summed in bfloat16 or wider, within the bound.
No kernel may reach another device: no remote copies, remote signals or barrier semaphores. Data moves between devices by JAX's collectives and lax.ppermute only.
A program may use at most 128 MiB of HBM per device.

v0:
```python
import jax
import jax.numpy as jnp
from jax import lax
from jax.sharding import PartitionSpec as P

epsilon_norm = 1e-05
discount = 1.0
trace_decay = 0.999
penalty_weight = 0.1


def joined(part, axis, combine):
    gathered = jax.tree.map(lambda a: lax.all_gather(a, axis), part)

    def take(source):
        return jax.tree.map(lambda a: lax.dynamic_index_in_dim(a, source, 0, False), gathered)

    return lax.fori_loop(
        1, lax.axis_size(axis), lambda source, state: combine(state, take(source)), take(0)
    )


def from_behind(value, axis, steps):
    count = lax.axis_size(axis)
    initial, last = (max(0, -steps), min(count, count - steps))
    return lax.ppermute(value, axis, [(source, source + steps) for source in range(initial, last)])


def normalize(rows, layers, exit_gains):
    states = rows.astype(jnp.float32)
    inverse = lax.rsqrt(jnp.mean(states * states, axis=-1, keepdims=True) + epsilon_norm)
    selector = (
        layers[:, None] == jnp.arange(exit_gains.shape[0], dtype=jnp.int32)[None, :]
    ).astype(jnp.float32)
    scaling = jnp.dot(selector, exit_gains, precision=lax.Precision.HIGHEST)
    return (states * inverse * scaling).astype(jnp.bfloat16)


def per_device(
    hidden, exit_layer, exit_gains, unembed, targets, values, rewards, ref_logprob, segment_end
):
    column_count = unembed.shape[1]
    column_start = lax.axis_index(("batch", "vocab")) * column_count
    columns = jnp.arange(column_count, dtype=jnp.int32)
    total_rows = targets.shape[0]
    owned = hidden.shape[0]
    peers = lax.axis_size("batch")
    width = hidden.shape[1]
    normed = normalize(hidden, exit_layer, exit_gains)
    gathered = lax.all_gather(normed, "batch", axis=0, tiled=True)
    block_rows = 512
    block_count = total_rows // block_rows

    def score_block(pair):
        rows_block, ids_block = pair
        logits = jnp.dot(rows_block, unembed, preferred_element_type=jnp.float32)
        row_max = jnp.max(logits, axis=1)
        row_total = jnp.sum(jnp.exp(logits - row_max[:, None]), axis=1)
        wanted = ids_block - column_start
        picked = jnp.sum(jnp.where(columns[None, :] == wanted[:, None], logits, 0.0), axis=1)
        return (row_max, row_total, picked)

    maxima, totals, picks = lax.map(
        score_block,
        (
            gathered.reshape(block_count, block_rows, width),
            targets.reshape(block_count, block_rows),
        ),
    )
    maxima = maxima.reshape(total_rows)
    totals = totals.reshape(total_rows)
    picks = picks.reshape(total_rows)
    maxima, totals, picks = (
        lax.all_to_all(maxima, "batch", split_axis=0, concat_axis=0, tiled=True),
        lax.all_to_all(totals, "batch", split_axis=0, concat_axis=0, tiled=True),
        lax.all_to_all(picks, "batch", split_axis=0, concat_axis=0, tiled=True),
    )
    maxima = maxima.reshape(peers, owned)
    totals = totals.reshape(peers, owned)
    picks = picks.reshape(peers, owned)
    group_max = jnp.max(maxima, axis=0)
    group_total = jnp.sum(totals * jnp.exp(maxima - group_max[None, :]), axis=0)
    group_pick = jnp.sum(picks, axis=0)

    def combine_groups(first, second):
        larger = jnp.maximum(first[0], second[0])
        summed = first[1] * jnp.exp(first[0] - larger) + second[1] * jnp.exp(second[0] - larger)
        return (larger, summed, first[2] + second[2])

    overall_max, overall_total, overall_pick = joined(
        (group_max, group_total, group_pick), "vocab", combine_groups
    )
    logprob = overall_pick - (overall_max + jnp.log(overall_total))
    following = from_behind(values[:1], "batch", -1)
    next_values = jnp.concatenate([values[1:], following])
    keeping = 1.0 - segment_end.astype(jnp.float32)
    shaped = rewards - penalty_weight * (logprob - ref_logprob)
    deltas = shaped + discount * next_values * keeping - values
    factors = discount * trace_decay * keeping

    def backward(running, inputs):
        factor, delta = inputs
        accrued = delta + factor * running[0]
        product = factor * running[1]
        return ((accrued, product), (accrued, product))

    finished, outputs = lax.scan(
        backward,
        (jnp.zeros((), jnp.float32), jnp.ones((), jnp.float32)),
        (factors, deltas),
        reverse=True,
    )
    local_adv, products = outputs
    head_adv = local_adv[:1]
    head_prod = products[:1]

    def relay_step(index, inbound):
        return from_behind(head_adv + head_prod * inbound, "batch", -1)

    incoming = lax.fori_loop(0, peers - 1, relay_step, jnp.zeros((1,), jnp.float32))
    advantages = local_adv + products * incoming
    return (logprob, advantages)


def solution(mesh):
    placed = (
        P("batch", None),
        P("batch"),
        P(),
        P(None, ("batch", "vocab")),
        P(),
        P("batch"),
        P("batch"),
        P("batch"),
        P("batch"),
    )
    return jax.shard_map(
        per_device, mesh=mesh, in_specs=placed, out_specs=(P("batch"), P("batch")), check_vma=False
    )
```

profile of v0, /device:TPU:1, one launch (start us, length us, event | category | flops | bytes accessed | tf_op | source)
XLA Modules:
  0.0 659.9 jit_solution(1969965212118673331)
XLA Ops:
  7.2 1.5 fusion.14
  8.8 3.4 fusion.13
  12.2 0.7 reshape.52
  12.9 83.9 %all-gather.8.cloned.1.call-done = bf16[1024,4096]{1,0:T(8,128)(2,1)} async-done(((bf16[128,4096]{1,0:T(8,128)(2,1)}), bf16[1024,4096]{1,0:T(8,128)(2,1)}) %all-gather.8.cloned.1.call-update) | async-done | bytes 8388624 | tf_op jit(solution)/shard_map/all_gather | solution.py:50
  96.8 49.9 %while.67 = (s32[]{:T(128)}, f32[2,512]{1,0:T(2,128)S(1)}, f32[2,512]{1,0:T(2,128)S(1)}, f32[2,512]{1,0:T(2,128)S(1)}, bf16[2,512,4096]{2,1,0:T(8,128)(2,1)}, /*...) while((s32[]{:T(128)}, f32[2,512]{1,0:T(2,128)S(1)}, ...), condition=%wide.region_5.6_spmd.clone, body=%wide.region_1.5_spmd.clone.sunk | while | flops 16823081984 | bytes 53471864 | solution.py:63
  96.9 22.6 %fusion.28 = (f32[512]{0:T(512)S(1)}, f32[512,4008]{0,1:T(8,128)S(1)}) fusion(bf16[4096,4008]{0,1:T(8,128)(2,1)} %get-tuple-element.681, bf16[2,512,4096]{2,1,0:T(8,128)(2,1)} %get-tuple-element.680, s32[]{:T(128)} %get-tuple-element.666), kind=kOutput, calls=%fused_computation.38.clone.1 | convolution fusion | flops 16812822528 | bytes 45238784 | tf_op jit(solution)/shard_map/while/body/eval_jaxpr/dot_general | solution.py:56
  119.5 2.2 select_reduce_fusion.2
  121.8 22.6 %fusion.28 = (f32[512]{0:T(512)S(1)}, f32[512,4008]{0,1:T(8,128)S(1)}) fusion(bf16[4096,4008]{0,1:T(8,128)(2,1)} %get-tuple-element.681, bf16[2,512,4096]{2,1,0:T(8,128)(2,1)} %get-tuple-element.680, s32[]{:T(128)} %get-tuple-element.666), kind=kOutput, calls=%fused_computation.38.clone.1 | convolution fusion | flops 16812822528 | bytes 45238784 | tf_op jit(solution)/shard_map/while/body/eval_jaxpr/dot_general | solution.py:56
  144.4 2.2 select_reduce_fusion.2
  147.3 3.4 all-to-all-start
  151.4 4.3 all-to-all-done
  155.7 3.9 all-to-all-start.1
  159.6 2.0 collective-permute-start.1
  162.3 2.2 all-to-all-done.1
  164.5 3.9 all-to-all-start.2
  168.4 5.9 all-gather.4
  174.3 5.9 all-gather.5
  180.2 5.0 all-gather.3
  185.3 1.1 fusion.17
  186.4 421.8 %while.65 = (s32[]{:T(128)}, f32[]{:T(128)}, f32[]{:T(128)}, f32[128]{0:T(128)S(1)}, f32[128]{0:T(128)S(1)}, /*index=5*/f32[128]{0:T(128)S(1)}, f32[128]{0:T(128)S(1)}, s32[]{:T(128)}, s32[]{:T(128)}) while((s32[]{:T(128)}, f32[]{:T(128)}, f32[]{:T(128)}, f32[128]{0:T(128)S(1)}, f32[128]{0:T(128)S(1)}, /*index=5*/f32[128]{0:T(128)S(1)}, ...), condition=%wide.region_12.13_spmd, body=%wide.region_11.12_spmd.sunk | while | flops 6 | bytes 189 | solution.py:107
  189.7 0.6 dynamic_slice.106
  196.3 0.6 dynamic_slice.106
  199.6 0.6 dynamic_slice.106
  202.9 0.6 dynamic_slice.106
  206.2 0.6 dynamic_slice.106
  209.5 0.6 dynamic_slice.106
  212.8 0.6 dynamic_slice.106
  216.1 0.6 dynamic_slice.106
  219.4 0.6 dynamic_slice.106
  222.7 0.6 dynamic_slice.106
  226.0 0.6 dynamic_slice.106
  229.3 0.6 dynamic_slice.106
  232.6 0.6 dynamic_slice.106
  239.2 0.6 dynamic_slice.106
  242.5 0.6 dynamic_slice.106
  245.7 0.6 dynamic_slice.106
  249.0 0.6 dynamic_slice.106
  252.3 0.6 dynamic_slice.106
  258.9 0.6 dynamic_slice.106
  262.2 0.6 dynamic_slice.106
  265.5 0.6 dynamic_slice.106
  268.8 0.6 dynamic_slice.106
  272.1 0.6 dynamic_slice.106
  275.4 0.6 dynamic_slice.106
  278.7 0.6 dynamic_slice.106
  282.0 0.6 dynamic_slice.106
  285.3 0.6 dynamic_slice.106
  288.6 0.6 dynamic_slice.106
  291.9 0.6 dynamic_slice.106
  608.2 44.3 %while.66 = (s32[]{:T(128)}, f32[1]{0:T(128)}, f32[1]{0:T(128)S(1)}, f32[1]{0:T(128)S(1)}, s32[]{:T(128)}) while((s32[]{:T(128)}, f32[1]{0:T(128)}, f32[1]{0:T(128)S(1)}, f32[1]{0:T(128)S(1)}, s32[]{:T(128)}) %tuple.128), condition=%wide.region_14.15_spmd, body=%wide.region_13.14_spmd.sunk | while | flops 4 | bytes 141 | solution.py:120
  608.3 9.0 %collective-permute-start = (f32[1]{0:T(128)}, f32[1]{0:T(128)}, u32[]{:S(2)}, u32[]{:S(2)}) collective-permute-start(f32[1]{0:T(128)} %add.147), channel_id=1, source_target_pairs={{4,0},{8,4},{12,8},{16,12},{20,16},{24,20},{28,24},{5,1},{9,5},{13... | collective-permute-start | bytes 20 | tf_op jit(solution)/shard_map/while/body/eval_jaxpr/ppermute | solution.py:26
  617.3 1.8 collective-permute-done
  619.8 2.9 collective-permute-start
  622.6 2.0 collective-permute-done
  625.2 2.9 collective-permute-start
  628.1 2.0 collective-permute-done
  630.7 2.9 collective-permute-start
  633.6 2.0 collective-permute-done
  636.2 2.9 collective-permute-start
  639.1 2.0 collective-permute-done
  641.7 2.9 collective-permute-start
  644.5 2.0 collective-permute-done
  647.2 2.9 collective-permute-start
  650.0 2.0 collective-permute-done
  (526 shorter events, 169.7 us)
Async XLA Ops:
  7.2 1.6 copy-start
  7.2 89.7 %all-gather.8.cloned.1.call-start = ((), (), s32[]{:S(2)}) async-start(), calls=%async_computation.3 | async-start | bytes 9437184 | tf_op jit(solution)/shard_map/all_gather | solution.py:50
  96.8 62.7 %copy-start.1 = (f32[128]{0:T(128)S(1)}, f32[128]{0:T(128)}, u32[]{:S(2)}) copy-start(f32[128]{0:T(128)} %param.22) | copy-start | bytes 1540
  96.8 88.4 %copy-start.2 = (f32[128]{0:T(128)S(1)}, f32[128]{0:T(128)}, u32[]{:S(2)}) copy-start(f32[128]{0:T(128)} %param.23) | copy-start | bytes 1540
  96.8 88.4 %copy-start.3 = (f32[128]{0:T(128)S(1)}, f32[128]{0:T(128)}, u32[]{:S(2)}) copy-start(f32[128]{0:T(128)} %param.24) | copy-start | bytes 1540
  96.8 88.4 %copy-start.4 = (s32[128]{0:T(128)S(1)}, s32[128]{0:T(128)}, u32[]{:S(2)}) copy-start(s32[128]{0:T(128)} %param.25) | copy-start | bytes 1540
  147.3 8.4 %all-to-all-start = ((f32[8,128,1]{1,2,0:T(1,128)}), f32[8,128,1]{1,2,0:T(1,128)S(1)}, u32[]{:S(2)}, u32[]{:S(2)}) async-start(f32[8,128,1]{1,2,0:T(1,128)} %all_to_all.18), calls=%async_computation | async-start | bytes 8192 | tf_op jit(solution)/shard_map/all_to_all | solution.py:74
  155.7 8.8 %all-to-all-start.1 = ((f32[8,128,1]{1,2,0:T(1,128)}), f32[8,128,1]{1,2,0:T(1,128)S(1)}, u32[]{:S(2)}, u32[]{:S(2)}) async-start(f32[8,128,1]{1,2,0:T(1,128)} %all_to_all.20), calls=%async_computation.1 | async-start | bytes 8192 | tf_op jit(solution)/shard_map/all_to_all | solution.py:75
  159.6 25.7 %collective-permute-start.1 = (f32[1]{0:T(128)S(1)}, f32[1]{0:T(128)}, u32[]{:S(2)}, u32[]{:S(2)}) collective-permute-start(f32[1]{0:T(128)S(1)} %bitcast.85), channel_id=1, source_target_pairs={{4,0},{8,4},{12,8},{16,12},{20,16},{24,20},{28,24},{5,1},{9,5},{13... | collective-permute-start | bytes 20 | tf_op jit(solution)/shard_map/ppermute | solution.py:26
  164.5 9.8 %all-to-all-start.2 = ((f32[8,128,1]{1,2,0:T(1,128)}), f32[8,128,1]{1,2,0:T(1,128)S(1)}, u32[]{:S(2)}, u32[]{:S(2)}) async-start(f32[8,128,1]{1,2,0:T(1,128)} %all_to_all.22), calls=%async_computation.2 | async-start | bytes 8192 | tf_op jit(solution)/shard_map/all_to_all | solution.py:76
  608.3 10.8 %collective-permute-start = (f32[1]{0:T(128)}, f32[1]{0:T(128)}, u32[]{:S(2)}, u32[]{:S(2)}) collective-permute-start(f32[1]{0:T(128)} %add.147), channel_id=1, source_target_pairs={{4,0},{8,4},{12,8},{16,12},{20,16},{24,20},{28,24},{5,1},{9,5},{13... | collective-permute-start | bytes 20 | tf_op jit(solution)/shard_map/while/body/eval_jaxpr/ppermute | solution.py:26
  619.8 4.8 collective-permute-start
  625.2 4.8 collective-permute-start
  630.7 4.8 collective-permute-start
  636.2 4.8 collective-permute-start
  641.7 4.8 collective-permute-start
  647.2 4.8 collective-permute-start
Sparse Core Ops, SparseCore 0:
  12.3 84.4 all-gather.7
where the time goes:
time: 664 us; the launch traced here: 660 us
  loops' own time  242 us (36%)
  local copies, waits for them, and re-layouts  187 us (28%)
  waiting for transfers between devices  104 us (16%)
  matrix products  48.5 us (7%)
  starting transfers between devices  39.4 us (6%)
  blocking collectives  16.7 us (3%)
  between operations  14.1 us (2%)
  other arithmetic  7.76 us (1%)
    another operation x1, loops' own time, per_device(): lax.scan(backward, (jnp.zeros((), jnp.float32), jnp.ones((), jnp.float32)...  237 us
    dynamic_slice x256, local copies, waits for them, and re-layouts, per_device(): lax.scan(backward, (jnp.zeros((), jnp.float32), jnp.ones((), jnp.float32)...  155 us
    all_gather x1, waiting for transfers between devices, per_device(): gathered = lax.all_gather(normed, 'batch', axis=0, tiled=True)  83.9 us
    dot_general x2, matrix products, score_block(): logits = jnp.dot(rows_block, unembed, preferred_element_type=jnp.float32)  45.2 us
    dynamic_update_slice x256, local copies, waits for them, and re-layouts, per_device(): lax.scan(backward, (jnp.zeros((), jnp.float32), jnp.ones((), jnp.float32)...  29.4 us
    ppermute x8, starting transfers between devices, from_behind(): lax.ppermute(value, axis, [(source, source + steps) for source in range(i...  28.2 us
    all_gather x3, blocking collectives, joined(): gathered = jax.tree.map(lambda a: lax.all_gather(a, axis), part)  16.7 us
    ppermute x8, waiting for transfers between devices, from_behind(): lax.ppermute(value, axis, [(source, source + steps) for source in range(i...  13.7 us
  transfers between devices with their start and end apart: 12, of which 10 were waited for; matrix products, arithmetic and copies ran while one was open for 0% of the time, Pallas kernels for 0%

commit v1 on v0

--- a/solution.py
+++ b/solution.py
@@ -2,11 +2,38 @@
 import jax.numpy as jnp
 from jax import lax
 from jax.sharding import PartitionSpec as P
+from jax.lax import axis_index, axis_size, ppermute
 
 epsilon_norm = 1e-05
 discount = 1.0
 trace_decay = 0.999
 penalty_weight = 0.1
+
+
+def thing_list(panel, dim_no):
+    panel = jnp.moveaxis(panel, 0, dim_no)
+    x_new = panel.shape
+    return panel.reshape(*x_new[:dim_no], x_new[dim_no] * x_new[dim_no + 1], *x_new[dim_no + 2 :])
+
+
+def rest_leaf(body, row_axis, d0):
+    how_many = axis_size(row_axis)
+    sides = []
+    for t in range(how_many):
+        sides.append((t, (t + 1) % how_many))
+    all_rows = []
+    for p, j0 in sides:
+        all_rows.append((j0, p))
+    f_next, v_next = ([], [])
+    for to_i in range(how_many - 1):
+        if to_i % 2 == 0:
+            f_next.append(ppermute(f_next[-1] if f_next else body, row_axis, sides))
+        else:
+            v_next.append(ppermute(v_next[-1] if v_next else body, row_axis, all_rows))
+    z1 = jnp.stack([*f_next[::-1], body, *v_next])
+    earlier = axis_index(row_axis) - len(f_next)
+    z1 = z1[(jnp.arange(how_many) - earlier) % how_many]
+    return thing_list(z1, d0)
 
 
 def joined(part, axis, combine):
@@ -47,7 +74,7 @@
     peers = lax.axis_size("batch")
     width = hidden.shape[1]
     normed = normalize(hidden, exit_layer, exit_gains)
-    gathered = lax.all_gather(normed, "batch", axis=0, tiled=True)
+    gathered = rest_leaf(normed, "batch", 0)
     block_rows = 512
     block_count = total_rows // block_rows
 

time: 664 us -> 694 us (1.045)
  starting transfers between devices: 39.4 us -> 76.8 us
  local copies, waits for them, and re-layouts: 187 us -> 213 us
  waiting for transfers between devices: 104 us -> 78.1 us
  between operations: 14.1 us -> 0.76 us
  loops' own time: 242 us -> 249 us
    all_gather x1 -> x0, waiting for transfers between devices: 83.9 us -> none  [per_device(): gathered = lax.all_gather(normed, 'batch', axis=0, tiled=True)]
    ppermute x0 -> x7, waiting for transfers between devices: none -> 56 us  [the longest x4 43.8 us: rest_leaf(): f_next.append(ppermute(f_next[-1] if f_next else body, row_axis, sides))]
    all_to_all x1, starting transfers between devices: 3.43 us -> 23.9 us  [per_device(): lax.all_to_all(maxima, 'batch', split_axis=0, concat_axis=0, tiled=True)]
    ppermute x0 -> x7, starting transfers between devices: none -> 17.8 us  [the longest x4 10.3 us: rest_leaf(): f_next.append(ppermute(f_next[-1] if f_next else body, row_axis, sides))]
    unnamed x10 -> x21, local copies, waits for them, and re-layouts: 0.02 us -> 12.5 us
    gather x0 -> x1, local copies, waits for them, and re-layouts: none -> 8.06 us  [rest_leaf(): z1 = z1[(jnp.arange(how_many) - earlier) % how_many]]
  transfers between devices with their start and end apart: 12 -> 18, of which waited for: 10 -> 16; matrix products, arithmetic and copies ran while one was open for 0% -> 2% of each run, Pallas kernels for 0% -> 0%
where the time goes in v1:
time: 694 us; the launch traced here: 690 us
  loops' own time  249 us (36%)
  local copies, waits for them, and re-layouts  213 us (31%)
  waiting for transfers between devices  78.1 us (11%)
  starting transfers between devices  76.8 us (11%)
  matrix products  47.5 us (7%)
  blocking collectives  16.6 us (2%)
  other arithmetic  7.78 us (1%)
    another operation x1, loops' own time, per_device(): lax.scan(backward, (jnp.zeros((), jnp.float32), jnp.ones((), jnp.float32)...  244 us
    dynamic_slice x256, local copies, waits for them, and re-layouts, per_device(): lax.scan(backward, (jnp.zeros((), jnp.float32), jnp.ones((), jnp.float32)...  160 us
    dot_general x2, matrix products, score_block(): logits = jnp.dot(rows_block, unembed, preferred_element_type=jnp.float32)  45.2 us
    ppermute x4, waiting for transfers between devices, rest_leaf(): f_next.append(ppermute(f_next[-1] if f_next else body, row_axis, sides))  43.8 us
    dynamic_update_slice x256, local copies, waits for them, and re-layouts, per_device(): lax.scan(backward, (jnp.zeros((), jnp.float32), jnp.ones((), jnp.float32)...  29.4 us
    ppermute x8, starting transfers between devices, from_behind(): lax.ppermute(value, axis, [(source, source + steps) for source in range(i...  27.3 us
    all_to_all x1, starting transfers between devices, per_device(): lax.all_to_all(maxima, 'batch', split_axis=0, concat_axis=0, tiled=True)  23.9 us
    all_gather x3, blocking collectives, joined(): gathered = jax.tree.map(lambda a: lax.all_gather(a, axis), part)  16.6 us
  transfers between devices with their start and end apart: 18, of which 16 were waited for; matrix products, arithmetic and copies ran while one was open for 2% of the time, Pallas kernels for 0%

profile of v1, /device:TPU:1, one launch (start us, length us, event | category | flops | bytes accessed | tf_op | source)
XLA Modules:
  0.0 689.9 jit_solution(4344166199350828798)
XLA Ops:
  0.6 1.6 fusion.14
  2.2 2.3 fusion.13
  4.5 2.7 collective-permute-start.1
  7.3 11.7 %collective-permute-done.1 = bf16[128,4096]{1,0:T(8,128)(2,1)S(1)} collective-permute-done((bf16[128,4096]{1,0:T(8,128)(2,1)S(1)}, bf16[128,4096]{1,0:T(8,128)(2,1)S(1)}, u32[]{:S(2)}, u32[]{:S(2)}) %collective-permute-start.1) | collective-permute-done | bytes 1048608 | tf_op jit(solution)/shard_map/ppermute | solution.py:30
  19.0 2.5 collective-permute-start.2
  21.6 19.0 %collective-permute-done.2 = bf16[128,4096]{1,0:T(8,128)(2,1)S(1)} collective-permute-done((bf16[128,4096]{1,0:T(8,128)(2,1)S(1)}, bf16[128,4096]{1,0:T(8,128)(2,1)S(1)}, u32[]{:S(2)}, u32[]{:S(2)}) %collective-permute-start.2) | collective-permute-done | bytes 1048608 | tf_op jit(solution)/shard_map/ppermute | solution.py:30
  40.6 2.5 collective-permute-start.3
  43.1 3.7 collective-permute-done.5
  46.8 2.3 collective-permute-start.6
  49.1 10.1 %collective-permute-done.3 = bf16[128,4096]{1,0:T(8,128)(2,1)} collective-permute-done((bf16[128,4096]{1,0:T(8,128)(2,1)S(1)}, bf16[128,4096]{1,0:T(8,128)(2,1)}, u32[]{:S(2)}, u32[]{:S(2)}) %collective-permute-start.3) | collective-permute-done | bytes 1048608 | tf_op jit(solution)/shard_map/ppermute | solution.py:30
  59.2 2.6 collective-permute-start.4
  61.8 0.7 reshape.97
  62.5 7.8 %collective-permute-done.6 = bf16[128,4096]{1,0:T(8,128)(2,1)} collective-permute-done((bf16[128,4096]{1,0:T(8,128)(2,1)S(1)}, bf16[128,4096]{1,0:T(8,128)(2,1)}, u32[]{:S(2)}, u32[]{:S(2)}) %collective-permute-start.6) | collective-permute-done | bytes 1048608 | tf_op jit(solution)/shard_map/ppermute | solution.py:32
  70.3 5.1 collective-permute-start.7
  75.4 2.9 collective-permute-done.4
  78.4 2.4 bitcast_dynamic-update-slice_fusion.7
  80.7 2.3 bitcast_dynamic-update-slice_fusion.6
  83.0 2.3 bitcast_dynamic-update-slice_fusion.5
  85.3 1.1 bitcast_dynamic-update-slice_fusion.4
  86.4 1.1 bitcast_dynamic-update-slice_fusion.3
  87.5 1.1 bitcast_dynamic-update-slice_fusion.2
  88.6 2.3 bitcast_dynamic-update-slice_fusion.1
  90.9 0.7 collective-permute-done.7
  91.5 1.0 bitcast_dynamic-update-slice_fusion
  92.6 8.1 %gather_fusion = bf16[8,128,4096]{2,1,0:T(8,128)(2,1)} fusion(bf16[8,128,4096]{2,1,0:T(8,128)(2,1)} %bitcast_dynamic-update-slice_fusion, s32[1024]{0:T(1024)S(1)} %pad_clamp_fusion), kind=kCustom, calls=%fused_computation | custom fusion | bytes 16777248 | tf_op jit(solution)/shard_map/gather | solution.py:35
  100.7 49.9 %while.67 = (s32[]{:T(128)}, f32[2,512]{1,0:T(2,128)S(1)}, f32[2,512]{1,0:T(2,128)S(1)}, f32[2,512]{1,0:T(2,128)S(1)}, bf16[2,512,4096]{2,1,0:T(8,128)(2,1)}, /*...) while((s32[]{:T(128)}, f32[2,512]{1,0:T(2,128)S(1)}, ...), condition=%wide.region_5.6_spmd.clone, body=%wide.region_1.5_spmd.clone.sunk | while | flops 16823081984 | bytes 53471864 | solution.py:90
  100.7 22.6 %fusion.30 = (f32[512]{0:T(512)S(1)}, f32[512,4008]{0,1:T(8,128)S(1)}) fusion(bf16[4096,4008]{0,1:T(8,128)(2,1)} %get-tuple-element.681, bf16[2,512,4096]{2,1,0:T(8,128)(2,1)} %get-tuple-element.680, s32[]{:T(128)} %get-tuple-element.666), kind=kOutput, calls=%fused_computation.54.clone.1 | convolution fusion | flops 16812822528 | bytes 45238784 | tf_op jit(solution)/shard_map/while/body/eval_jaxpr/dot_general | solution.py:83
  123.3 2.2 select_reduce_fusion.2
  125.6 22.6 %fusion.30 = (f32[512]{0:T(512)S(1)}, f32[512,4008]{0,1:T(8,128)S(1)}) fusion(bf16[4096,4008]{0,1:T(8,128)(2,1)} %get-tuple-element.681, bf16[2,512,4096]{2,1,0:T(8,128)(2,1)} %get-tuple-element.680, s32[]{:T(128)} %get-tuple-element.666), kind=kOutput, calls=%fused_computation.54.clone.1 | convolution fusion | flops 16812822528 | bytes 45238784 | tf_op jit(solution)/shard_map/while/body/eval_jaxpr/dot_general | solution.py:83
  148.2 2.2 select_reduce_fusion.2
  151.2 23.9 %all-to-all-start = ((f32[8,128,1]{1,2,0:T(1,128)}), f32[8,128,1]{1,2,0:T(1,128)S(1)}, u32[]{:S(2)}, u32[]{:S(2)}) async-start(f32[8,128,1]{1,2,0:T(1,128)} %all_to_all.18), calls=%async_computation | async-start | bytes 8192 | tf_op jit(solution)/shard_map/all_to_all | solution.py:101
  175.6 4.3 all-to-all-done
  180.0 3.9 all-to-all-start.1
  183.9 2.0 collective-permute-start.8
  186.6 2.2 all-to-all-done.1
  188.8 3.9 all-to-all-start.2
  192.7 5.8 all-gather.4
  198.5 5.9 all-gather.5
  204.4 4.9 all-gather.3
  209.5 1.1 fusion.19
  210.6 432.9 %while.65 = (s32[]{:T(128)}, f32[]{:T(128)}, f32[]{:T(128)}, f32[128]{0:T(128)S(1)}, f32[128]{0:T(128)S(1)}, /*index=5*/f32[128]{0:T(128)S(1)}, f32[128]{0:T(128)S(1)}, s32[]{:T(128)}, s32[]{:T(128)}) while((s32[]{:T(128)}, f32[]{:T(128)}, f32[]{:T(128)}, f32[128]{0:T(128)S(1)}, f32[128]{0:T(128)S(1)}, /*index=5*/f32[128]{0:T(128)S(1)}, ...), condition=%wide.region_12.13_spmd, body=%wide.region_11.12_spmd.sunk | while | flops 6 | bytes 189 | solution.py:134
  214.0 0.6 dynamic_slice.106
  217.4 0.6 dynamic_slice.106
  224.2 0.6 dynamic_slice.106
  227.5 0.6 dynamic_slice.106
  230.9 0.6 dynamic_slice.106
  237.7 0.6 dynamic_slice.106
  241.1 0.6 dynamic_slice.106
  244.4 0.6 dynamic_slice.106
  643.5 45.8 %while.66 = (s32[]{:T(128)}, f32[1]{0:T(128)}, f32[1]{0:T(128)S(1)}, f32[1]{0:T(128)S(1)}, s32[]{:T(128)}) while((s32[]{:T(128)}, f32[1]{0:T(128)}, f32[1]{0:T(128)S(1)}, f32[1]{0:T(128)S(1)}, s32[]{:T(128)}) %tuple.127), condition=%wide.region_14.15_spmd, body=%wide.region_13.14_spmd.sunk | while | flops 4 | bytes 141 | solution.py:147
  643.6 8.9 %collective-permute-start = (f32[1]{0:T(128)}, f32[1]{0:T(128)}, u32[]{:S(2)}, u32[]{:S(2)}) collective-permute-start(f32[1]{0:T(128)} %add.181), channel_id=1, source_target_pairs={{4,0},{8,4},{12,8},{16,12},{20,16},{24,20},{28,24},{5,1},{9,5},{13... | collective-permute-start | bytes 20 | tf_op jit(solution)/shard_map/while/body/eval_jaxpr/ppermute | solution.py:53
  652.5 2.1 collective-permute-done
  655.3 2.7 collective-permute-start
  658.0 2.3 collective-permute-done
  661.0 2.7 collective-permute-start
  663.7 2.3 collective-permute-done
  666.7 2.7 collective-permute-start
  669.4 2.3 collective-permute-done
  672.4 2.7 collective-permute-start
  675.1 2.3 collective-permute-done
  678.1 2.7 collective-permute-start
  680.8 2.3 collective-permute-done
  683.8 2.7 collective-permute-start
  686.5 2.3 collective-permute-done
  (552 shorter events, 187.0 us)
Async XLA Ops:
  0.6 1.6 copy-start
  4.5 14.5 %collective-permute-start.1 = (bf16[128,4096]{1,0:T(8,128)(2,1)S(1)}, bf16[128,4096]{1,0:T(8,128)(2,1)S(1)}, u32[]{:S(2)}, u32[]{:S(2)}) collective-permute-start(bf16[128,4096]{1,0:T(8,128)(2,1)S(1)} %fusion.13), channel_id=1, source_target_pairs={{0,4},{4,8},{8,12},{12,16},{16,20},{20,24},{24,28},{28,0},{1,5},{5... | collective-permute-start | bytes 3145736 | tf_op jit(solution)/shard_map/ppermute | solution.py:30
  19.0 21.6 %collective-permute-start.2 = (bf16[128,4096]{1,0:T(8,128)(2,1)S(1)}, bf16[128,4096]{1,0:T(8,128)(2,1)S(1)}, u32[]{:S(2)}, u32[]{:S(2)}) collective-permute-start(bf16[128,4096]{1,0:T(8,128)(2,1)S(1)} %collective-permute-done.1), channel_id=1, source_target_pairs={{0,4},{4,8},{8,12},{12,16},{16,20},{20,24},{24,28},{28,0},{1,5},{5... | collective-permute-start | bytes 3145736 | tf_op jit(solution)/shard_map/ppermute | solution.py:30
  21.5 25.3 %collective-permute-start.5 = (bf16[128,4096]{1,0:T(8,128)(2,1)S(1)}, bf16[128,4096]{1,0:T(8,128)(2,1)S(1)}, u32[]{:S(2)}, u32[]{:S(2)}) collective-permute-start(bf16[128,4096]{1,0:T(8,128)(2,1)S(1)} %fusion.13), channel_id=1, source_target_pairs={{4,0},{8,4},{12,8},{16,12},{20,16},{24,20},{28,24},{0,28},{5,1},{9... | collective-permute-start | bytes 3145736 | tf_op jit(solution)/shard_map/ppermute | solution.py:32
  40.6 6.2 copy-start.2
  40.6 18.6 %collective-permute-start.3 = (bf16[128,4096]{1,0:T(8,128)(2,1)S(1)}, bf16[128,4096]{1,0:T(8,128)(2,1)}, u32[]{:S(2)}, u32[]{:S(2)}) collective-permute-start(bf16[128,4096]{1,0:T(8,128)(2,1)S(1)} %collective-permute-done.2), channel_id=1, source_target_pairs={{0,4},{4,8},{8,12},{12,16},{16,20},{20,24},{24,28},{28,0},{1,5},{5... | collective-permute-start | bytes 3145736 | tf_op jit(solution)/shard_map/ppermute | solution.py:30
  46.8 23.5 %collective-permute-start.6 = (bf16[128,4096]{1,0:T(8,128)(2,1)S(1)}, bf16[128,4096]{1,0:T(8,128)(2,1)}, u32[]{:S(2)}, u32[]{:S(2)}) collective-permute-start(bf16[128,4096]{1,0:T(8,128)(2,1)S(1)} %collective-permute-done.5), channel_id=1, source_target_pairs={{4,0},{8,4},{12,8},{16,12},{20,16},{24,20},{28,24},{0,28},{5,1},{9... | collective-permute-start | bytes 3145736 | tf_op jit(solution)/shard_map/ppermute | solution.py:32
  59.2 19.2 %collective-permute-start.4 = (bf16[128,4096]{1,0:T(8,128)(2,1)}, bf16[128,4096]{1,0:T(8,128)(2,1)}, u32[]{:S(2)}, u32[]{:S(2)}) collective-permute-start(bf16[128,4096]{1,0:T(8,128)(2,1)} %collective-permute-done.3), channel_id=1, source_target_pairs={{0,4},{4,8},{8,12},{12,16},{16,20},{20,24},{24,28},{28,0},{1,5},{5... | collective-permute-start | bytes 3145736 | tf_op jit(solution)/shard_map/ppermute | solution.py:30
  70.3 21.2 %collective-permute-start.7 = (bf16[128,4096]{1,0:T(8,128)(2,1)}, bf16[128,4096]{1,0:T(8,128)(2,1)S(1)}, u32[]{:S(2)}, u32[]{:S(2)}) collective-permute-start(bf16[128,4096]{1,0:T(8,128)(2,1)} %collective-permute-done.6), channel_id=1, source_target_pairs={{4,0},{8,4},{12,8},{16,12},{20,16},{24,20},{28,24},{0,28},{5,1},{9... | collective-permute-start | bytes 3145736 | tf_op jit(solution)/shard_map/ppermute | solution.py:32
  100.6 83.2 %copy-start.3 = (f32[128]{0:T(128)S(1)}, f32[128]{0:T(128)}, u32[]{:S(2)}) copy-start(f32[128]{0:T(128)} %param.22) | copy-start | bytes 1540
  100.6 108.8 %copy-start.4 = (f32[128]{0:T(128)S(1)}, f32[128]{0:T(128)}, u32[]{:S(2)}) copy-start(f32[128]{0:T(128)} %param.23) | copy-start | bytes 1540
  100.6 108.8 %copy-start.5 = (f32[128]{0:T(128)S(1)}, f32[128]{0:T(128)}, u32[]{:S(2)}) copy-start(f32[128]{0:T(128)} %param.24) | copy-start | bytes 1540
  100.7 108.8 %copy-start.6 = (s32[128]{0:T(128)S(1)}, s32[128]{0:T(128)}, u32[]{:S(2)}) copy-start(s32[128]{0:T(128)} %param.25) | copy-start | bytes 1540
  150.5 539.4 %copy-start.1 = (f32[8,4096]{1,0:T(8,128)S(1)}, f32[8,4096]{1,0:T(8,128)}, u32[]{:S(2)}) copy-start(f32[8,4096]{1,0:T(8,128)} %param.19) | copy-start | bytes 393220
  151.2 28.8 %all-to-all-start = ((f32[8,128,1]{1,2,0:T(1,128)}), f32[8,128,1]{1,2,0:T(1,128)S(1)}, u32[]{:S(2)}, u32[]{:S(2)}) async-start(f32[8,128,1]{1,2,0:T(1,128)} %all_to_all.18), calls=%async_computation | async-start | bytes 8192 | tf_op jit(solution)/shard_map/all_to_all | solution.py:101
  180.0 8.8 %all-to-all-start.1 = ((f32[8,128,1]{1,2,0:T(1,128)}), f32[8,128,1]{1,2,0:T(1,128)S(1)}, u32[]{:S(2)}, u32[]{:S(2)}) async-start(f32[8,128,1]{1,2,0:T(1,128)} %all_to_all.20), calls=%async_computation.1 | async-start | bytes 8192 | tf_op jit(solution)/shard_map/all_to_all | solution.py:102
  183.9 25.6 %collective-permute-start.8 = (f32[1]{0:T(128)S(1)}, f32[1]{0:T(128)}, u32[]{:S(2)}, u32[]{:S(2)}) collective-permute-start(f32[1]{0:T(128)S(1)} %bitcast.104), channel_id=1, source_target_pairs={{4,0},{8,4},{12,8},{16,12},{20,16},{24,20},{28,24},{5,1},{9,5},{13... | collective-permute-start | bytes 20 | tf_op jit(solution)/shard_map/ppermute | solution.py:53
  188.8 9.7 %all-to-all-start.2 = ((f32[8,128,1]{1,2,0:T(1,128)}), f32[8,128,1]{1,2,0:T(1,128)S(1)}, u32[]{:S(2)}, u32[]{:S(2)}) async-start(f32[8,128,1]{1,2,0:T(1,128)} %all_to_all.22), calls=%async_computation.2 | async-start | bytes 8192 | tf_op jit(solution)/shard_map/all_to_all | solution.py:103
  643.6 11.0 %collective-permute-start = (f32[1]{0:T(128)}, f32[1]{0:T(128)}, u32[]{:S(2)}, u32[]{:S(2)}) collective-permute-start(f32[1]{0:T(128)} %add.181), channel_id=1, source_target_pairs={{4,0},{8,4},{12,8},{16,12},{20,16},{24,20},{28,24},{5,1},{9,5},{13... | collective-permute-start | bytes 20 | tf_op jit(solution)/shard_map/while/body/eval_jaxpr/ppermute | solution.py:53
  655.3 5.0 collective-permute-start
  661.0 5.0 collective-permute-start
  666.7 5.0 collective-permute-start
  672.4 5.0 collective-permute-start
  678.1 5.0 collective-permute-start
  683.8 5.0 collective-permute-start
